TPU v7x, 32 devices: a whole 2x2x4 slice. The times are simulated.
32 devices in a mesh: crow: 2 (over y), ccol: 8 (over z, x), half: 2 (over core).
Axes of the slice: x: 2, y: 2, z: 4, core: 2. Of those that a mesh axis runs over, the one named last changes fastest.
Arguments:
- operator: bfloat16 [2, 8, 2048, 2048], P('crow', 'ccol', 'half'), may hold values from -0.09375 to 0.09375
- east_sources: bfloat16 [2, 8, 384, 2048], P('crow', 'ccol', None, 'half'), may hold values from -6 to 6
- west_sources: bfloat16 [2, 8, 384, 2048], P('crow', 'ccol', None, 'half'), may hold values from -6 to 6
Outputs:
- east_traces: bfloat16 [2, 8, 384, 2048], P('crow', 'ccol', None, 'half')
- west_traces: bfloat16 [2, 8, 384, 2048], P('crow', 'ccol', None, 'half')
All inputs are finite; a program needn't handle non-finite values.
Results may differ from a plain program's by a relative error of at most 0.025.
Values may be sent and summed in bfloat16 or wider, within the bound.
A program may use at most 64 MiB of HBM per device.

v0:
```python
import jax
import jax.numpy as jnp
from jax import lax
from jax.sharding import PartitionSpec as P


def shifted(shard, axis, by):
    length = lax.axis_size(axis)
    pairs = [(i, i + by) for i in range(length) if 0 <= i + by < length]
    return lax.ppermute(shard, axis, pairs)


def local(operator, east_sources, west_sources):
    matrix = operator[0, 0]
    east_source = east_sources[0, 0]
    west_source = west_sources[0, 0]
    batch_rows, half_width = east_source.shape
    full_width = matrix.shape[1]
    rows_count = lax.axis_size("crow")
    cols_count = lax.axis_size("ccol")
    row_index = lax.axis_index("crow")
    col_index = lax.axis_index("ccol")
    block_count = 8
    block_rows = batch_rows // block_count
    step_count = rows_count + cols_count - 1 + block_count - 1
    east_level = row_index + col_index
    west_level = rows_count - 1 - row_index + (cols_count - 1 - col_index)

    def east_product(inflow, active):
        running = jnp.zeros((block_rows, half_width), jnp.float32)
        segment = lax.all_gather(inflow, "half", axis=1, tiled=True)
        return lax.cond(
            active,
            lambda: lax.dot_general(
                segment, matrix, (((1,), (1,)), ((), ())), preferred_element_type=jnp.float32
            ),
            lambda: running,
        )

    def west_product(inflow, active):
        partial_value = lax.cond(
            active,
            lambda: jnp.dot(inflow, matrix, preferred_element_type=jnp.float32),
            lambda: jnp.zeros((block_rows, full_width), jnp.float32),
        )
        return lax.psum_scatter(partial_value, "half", scatter_dimension=1, tiled=True)

    empty_block = jnp.zeros((block_rows, half_width), jnp.bfloat16)

    def place(result, newest, active, clamped):
        older = lax.dynamic_slice_in_dim(result, clamped * block_rows, block_rows, 0)
        kept = jnp.where(active, newest, older)
        return lax.dynamic_update_slice_in_dim(result, kept, clamped * block_rows, 0)

    def east_step(step_no, carry_state):
        previous, result = carry_state
        from_north = shifted(previous, "crow", 1)
        from_west = shifted(previous, "ccol", 1)
        inflow = (from_north.astype(jnp.float32) + from_west.astype(jnp.float32)).astype(
            jnp.bfloat16
        )
        block_index = step_no - east_level
        active = (block_index >= 0) & (block_index < block_count)
        clamped = jnp.clip(block_index, 0, block_count - 1)
        product = east_product(inflow, active)
        source = lax.dynamic_slice_in_dim(east_source, clamped * block_rows, block_rows, 0)
        newest = (product + source.astype(jnp.float32)).astype(jnp.bfloat16)
        newest = jnp.where(active, newest, empty_block)
        return (newest, place(result, newest, active, clamped))

    def west_step(step_no, carry_state):
        previous, result = carry_state
        from_south = shifted(previous, "crow", -1)
        from_east = shifted(previous, "ccol", -1)
        inflow = (from_south.astype(jnp.float32) + from_east.astype(jnp.float32)).astype(
            jnp.bfloat16
        )
        block_index = step_no - west_level
        active = (block_index >= 0) & (block_index < block_count)
        clamped = jnp.clip(block_index, 0, block_count - 1)
        summed = west_product(inflow, active)
        source = lax.dynamic_slice_in_dim(west_source, clamped * block_rows, block_rows, 0)
        newest = (summed + source.astype(jnp.float32)).astype(jnp.bfloat16)
        newest = jnp.where(active, newest, empty_block)
        return (newest, place(result, newest, active, clamped))

    start_east = (empty_block, jnp.zeros((block_count * block_rows, half_width), jnp.bfloat16))
    start_west = (empty_block, jnp.zeros((block_count * block_rows, half_width), jnp.bfloat16))

    def both_steps(step_no, states):
        return (east_step(step_no, states[0]), west_step(step_no, states[1]))

    east_final, west_final = lax.fori_loop(0, step_count, both_steps, (start_east, start_west))
    east_result = east_final[1]
    west_result = west_final[1]
    return (east_result[None, None], west_result[None, None])


def solution(mesh):
    in_specs = (
        P("crow", "ccol", "half", None),
        P("crow", "ccol", None, "half"),
        P("crow", "ccol", None, "half"),
    )
    out_specs = (P("crow", "ccol", None, "half"), P("crow", "ccol", None, "half"))
    return jax.shard_map(local, mesh=mesh, in_specs=in_specs, out_specs=out_specs, check_vma=False)
```

profile of v0, /device:TPU:0, one launch (start us, length us, event | category | flops | bytes accessed | tf_op | source)
XLA Modules:
  0.0 475.3 jit_solution(4178138326142489728)
XLA Ops:
  7.4 460.3 %while.20 = (s32[]{:T(128)}, bf16[48,1024]{1,0:T(8,128)(2,1)S(1)}, bf16[384,1024]{1,0:T(8,128)(2,1)S(1)}, bf16[48,1024]{1,0:T(8,128)(2,1)S(1)}, bf16[384,1024]{1...) while((s32[]{:T(128)}, bf16[48,1024]{1,0:T(8,128)(2,1)S(1)}, ...), condition=%wide.region_6.7_spmd.clone, body=%wide.region_0.6_spmd.clone.sunk | while | flops 403636224 | bytes 16646806 | solution.py:93
  10.1 4.5 collective-permute-done.3
  17.3 4.4 collective-permute-start.1
  21.7 4.8 %collective-permute-start = (bf16[48,1024]{1,0:T(8,128)(2,1)S(1)}, bf16[48,1024]{1,0:T(8,128)(2,1)S(1)}, u32[]{:S(2)}, u32[]{:S(2)}) collective-permute-start(bf16[48,1024]{1,0:T(8,128)(2,1)S(1)} %broadcast_select_fusion.4), channel_id=1, source_target_pairs={{0,2},{2,4},{4,6},{6,8},{8,10},{10,12},{12,14},{1,3},{3,5},{5,7},{... | collective-permute-start | bytes 294920 | tf_op jit(solution)/shard_map/while/body/eval_jaxpr/ppermute | solution.py:10
  45.3 4.3 collective-permute-start.1
  75.0 4.6 collective-permute-start
  103.3 4.6 collective-permute-start
  131.6 4.6 collective-permute-start
  160.0 4.6 collective-permute-start
  181.2 4.6 collective-permute-done.2
  191.0 8.2 %collective-permute-start = (bf16[48,1024]{1,0:T(8,128)(2,1)S(1)}, bf16[48,1024]{1,0:T(8,128)(2,1)S(1)}, u32[]{:S(2)}, u32[]{:S(2)}) collective-permute-start(bf16[48,1024]{1,0:T(8,128)(2,1)S(1)} %broadcast_select_fusion.4), channel_id=1, source_target_pairs={{0,2},{2,4},{4,6},{6,8},{8,10},{10,12},{12,14},{1,3},{3,5},{5,7},{... | collective-permute-start | bytes 294920 | tf_op jit(solution)/shard_map/while/body/eval_jaxpr/ppermute | solution.py:10
  218.6 7.3 %collective-permute-start.1 = (bf16[48,1024]{1,0:T(8,128)(2,1)S(1)}, bf16[48,1024]{1,0:T(8,128)(2,1)S(1)}, u32[]{:S(2)}, u32[]{:S(2)}) collective-permute-start(bf16[48,1024]{1,0:T(8,128)(2,1)S(1)} %broadcast_select_fusion.4), channel_id=1, source_target_pairs={{0,16},{1,17},{2,18},{3,19},{4,20},{5,21},{6,22},{7,23},{8,24},{9,... | collective-permute-start | bytes 294920 | tf_op jit(solution)/shard_map/while/body/eval_jaxpr/ppermute | solution.py:10
  225.9 4.6 collective-permute-start
  257.2 4.6 collective-permute-start
  270.7 4.7 collective-permute-done.3
  275.4 4.9 %collective-permute-done.2 = bf16[48,1024]{1,0:T(8,128)(2,1)S(1)} collective-permute-done((bf16[48,1024]{1,0:T(8,128)(2,1)S(1)}, bf16[48,1024]{1,0:T(8,128)(2,1)S(1)}, u32[]{:S(2)}, u32[]{:S(2)}) %collective-permute-start.2) | collective-permute-done | bytes 98336 | tf_op jit(solution)/shard_map/while/body/eval_jaxpr/ppermute | solution.py:10
  288.5 4.6 collective-permute-start
  312.0 4.8 %collective-permute-start.1 = (bf16[48,1024]{1,0:T(8,128)(2,1)S(1)}, bf16[48,1024]{1,0:T(8,128)(2,1)S(1)}, u32[]{:S(2)}, u32[]{:S(2)}) collective-permute-start(bf16[48,1024]{1,0:T(8,128)(2,1)S(1)} %broadcast_select_fusion.4), channel_id=1, source_target_pairs={{0,16},{1,17},{2,18},{3,19},{4,20},{5,21},{6,22},{7,23},{8,24},{9,... | collective-permute-start | bytes 294920 | tf_op jit(solution)/shard_map/while/body/eval_jaxpr/ppermute | solution.py:10
  316.9 7.6 %collective-permute-start = (bf16[48,1024]{1,0:T(8,128)(2,1)S(1)}, bf16[48,1024]{1,0:T(8,128)(2,1)S(1)}, u32[]{:S(2)}, u32[]{:S(2)}) collective-permute-start(bf16[48,1024]{1,0:T(8,128)(2,1)S(1)} %broadcast_select_fusion.4), channel_id=1, source_target_pairs={{0,2},{2,4},{4,6},{6,8},{8,10},{10,12},{12,14},{1,3},{3,5},{5,7},{... | collective-permute-start | bytes 294920 | tf_op jit(solution)/shard_map/while/body/eval_jaxpr/ppermute | solution.py:10
  347.6 5.2 %collective-permute-start = (bf16[48,1024]{1,0:T(8,128)(2,1)S(1)}, bf16[48,1024]{1,0:T(8,128)(2,1)S(1)}, u32[]{:S(2)}, u32[]{:S(2)}) collective-permute-start(bf16[48,1024]{1,0:T(8,128)(2,1)S(1)} %broadcast_select_fusion.4), channel_id=1, source_target_pairs={{0,2},{2,4},{4,6},{6,8},{8,10},{10,12},{12,14},{1,3},{3,5},{5,7},{... | collective-permute-start | bytes 294920 | tf_op jit(solution)/shard_map/while/body/eval_jaxpr/ppermute | solution.py:10
  365.8 4.3 collective-permute-done.2
  378.3 5.2 %collective-permute-start = (bf16[48,1024]{1,0:T(8,128)(2,1)S(1)}, bf16[48,1024]{1,0:T(8,128)(2,1)S(1)}, u32[]{:S(2)}, u32[]{:S(2)}) collective-permute-start(bf16[48,1024]{1,0:T(8,128)(2,1)S(1)} %broadcast_select_fusion.4), channel_id=1, source_target_pairs={{0,2},{2,4},{4,6},{6,8},{8,10},{10,12},{12,14},{1,3},{3,5},{5,7},{... | collective-permute-start | bytes 294920 | tf_op jit(solution)/shard_map/while/body/eval_jaxpr/ppermute | solution.py:10
  406.7 5.1 %collective-permute-start = (bf16[48,1024]{1,0:T(8,128)(2,1)S(1)}, bf16[48,1024]{1,0:T(8,128)(2,1)S(1)}, u32[]{:S(2)}, u32[]{:S(2)}) collective-permute-start(bf16[48,1024]{1,0:T(8,128)(2,1)S(1)} %broadcast_select_fusion.4), channel_id=1, source_target_pairs={{0,2},{2,4},{4,6},{6,8},{8,10},{10,12},{12,14},{1,3},{3,5},{5,7},{... | collective-permute-start | bytes 294920 | tf_op jit(solution)/shard_map/while/body/eval_jaxpr/ppermute | solution.py:10
  456.9 4.6 collective-permute-start
  (369 shorter events, 395.0 us)
Async XLA Ops:
  7.4 27.8 %reduce-scatter.2.cloned.1.call-start = ((), (), s32[]{:S(2)}) async-start(), calls=%async_computation.1 | async-start | bytes 589824 | tf_op jit(solution)/shard_map/while/body/eval_jaxpr/reduce_scatter | solution.py:46
  36.3 23.7 %reduce-scatter.2.cloned.1.call-start = ((), (), s32[]{:S(2)}) async-start(), calls=%async_computation.1 | async-start | bytes 589824 | tf_op jit(solution)/shard_map/while/body/eval_jaxpr/reduce_scatter | solution.py:46
  61.1 27.2 %reduce-scatter.2.cloned.1.call-start = ((), (), s32[]{:S(2)}) async-start(), calls=%async_computation.1 | async-start | bytes 589824 | tf_op jit(solution)/shard_map/while/body/eval_jaxpr/reduce_scatter | solution.py:46
  89.4 27.2 %reduce-scatter.2.cloned.1.call-start = ((), (), s32[]{:S(2)}) async-start(), calls=%async_computation.1 | async-start | bytes 589824 | tf_op jit(solution)/shard_map/while/body/eval_jaxpr/reduce_scatter | solution.py:46
  117.7 27.2 %reduce-scatter.2.cloned.1.call-start = ((), (), s32[]{:S(2)}) async-start(), calls=%async_computation.1 | async-start | bytes 589824 | tf_op jit(solution)/shard_map/while/body/eval_jaxpr/reduce_scatter | solution.py:46
  146.0 27.3 %reduce-scatter.2.cloned.1.call-start = ((), (), s32[]{:S(2)}) async-start(), calls=%async_computation.1 | async-start | bytes 589824 | tf_op jit(solution)/shard_map/while/body/eval_jaxpr/reduce_scatter | solution.py:46
  174.4 33.5 %reduce-scatter.2.cloned.1.call-start = ((), (), s32[]{:S(2)}) async-start(), calls=%async_computation.1 | async-start | bytes 589824 | tf_op jit(solution)/shard_map/while/body/eval_jaxpr/reduce_scatter | solution.py:46
  175.7 10.1 %collective-permute-start.2 = (bf16[48,1024]{1,0:T(8,128)(2,1)S(1)}, bf16[48,1024]{1,0:T(8,128)(2,1)S(1)}, u32[]{:S(2)}, u32[]{:S(2)}) collective-permute-start(bf16[48,1024]{1,0:T(8,128)(2,1)S(1)} %broadcast_select_fusion.5), channel_id=1, source_target_pairs={{2,0},{4,2},{6,4},{8,6},{10,8},{12,10},{14,12},{3,1},{5,3},{7,5},{... | collective-permute-start | bytes 294920 | tf_op jit(solution)/shard_map/while/body/eval_jaxpr/ppermute | solution.py:10
  186.7 12.5 %collective-permute-start.1 = (bf16[48,1024]{1,0:T(8,128)(2,1)S(1)}, bf16[48,1024]{1,0:T(8,128)(2,1)S(1)}, u32[]{:S(2)}, u32[]{:S(2)}) collective-permute-start(bf16[48,1024]{1,0:T(8,128)(2,1)S(1)} %broadcast_select_fusion.4), channel_id=1, source_target_pairs={{0,16},{1,17},{2,18},{3,19},{4,20},{5,21},{6,22},{7,23},{8,24},{9,... | collective-permute-start | bytes 294920 | tf_op jit(solution)/shard_map/while/body/eval_jaxpr/ppermute | solution.py:10
  191.0 10.4 %collective-permute-start = (bf16[48,1024]{1,0:T(8,128)(2,1)S(1)}, bf16[48,1024]{1,0:T(8,128)(2,1)S(1)}, u32[]{:S(2)}, u32[]{:S(2)}) collective-permute-start(bf16[48,1024]{1,0:T(8,128)(2,1)S(1)} %broadcast_select_fusion.4), channel_id=1, source_target_pairs={{0,2},{2,4},{4,6},{6,8},{8,10},{10,12},{12,14},{1,3},{3,5},{5,7},{... | collective-permute-start | bytes 294920 | tf_op jit(solution)/shard_map/while/body/eval_jaxpr/ppermute | solution.py:10
  208.9 30.2 %reduce-scatter.2.cloned.1.call-start = ((), (), s32[]{:S(2)}) async-start(), calls=%async_computation.1 | async-start | bytes 589824 | tf_op jit(solution)/shard_map/while/body/eval_jaxpr/reduce_scatter | solution.py:46
  218.6 11.9 %collective-permute-start.1 = (bf16[48,1024]{1,0:T(8,128)(2,1)S(1)}, bf16[48,1024]{1,0:T(8,128)(2,1)S(1)}, u32[]{:S(2)}, u32[]{:S(2)}) collective-permute-start(bf16[48,1024]{1,0:T(8,128)(2,1)S(1)} %broadcast_select_fusion.4), channel_id=1, source_target_pairs={{0,16},{1,17},{2,18},{3,19},{4,20},{5,21},{6,22},{7,23},{8,24},{9,... | collective-permute-start | bytes 294920 | tf_op jit(solution)/shard_map/while/body/eval_jaxpr/ppermute | solution.py:10
  240.3 26.7 %reduce-scatter.2.cloned.1.call-start = ((), (), s32[]{:S(2)}) async-start(), calls=%async_computation.1 | async-start | bytes 589824 | tf_op jit(solution)/shard_map/while/body/eval_jaxpr/reduce_scatter | solution.py:46
  268.0 30.2 %reduce-scatter.2.cloned.1.call-start = ((), (), s32[]{:S(2)}) async-start(), calls=%async_computation.1 | async-start | bytes 589824 | tf_op jit(solution)/shard_map/while/body/eval_jaxpr/reduce_scatter | solution.py:46
  269.4 11.0 %collective-permute-start.2 = (bf16[48,1024]{1,0:T(8,128)(2,1)S(1)}, bf16[48,1024]{1,0:T(8,128)(2,1)S(1)}, u32[]{:S(2)}, u32[]{:S(2)}) collective-permute-start(bf16[48,1024]{1,0:T(8,128)(2,1)S(1)} %broadcast_select_fusion.5), channel_id=1, source_target_pairs={{2,0},{4,2},{6,4},{8,6},{10,8},{12,10},{14,12},{3,1},{5,3},{7,5},{... | collective-permute-start | bytes 294920 | tf_op jit(solution)/shard_map/while/body/eval_jaxpr/ppermute | solution.py:10
  299.4 30.2 %reduce-scatter.2.cloned.1.call-start = ((), (), s32[]{:S(2)}) async-start(), calls=%async_computation.1 | async-start | bytes 589824 | tf_op jit(solution)/shard_map/while/body/eval_jaxpr/reduce_scatter | solution.py:46
  312.0 12.4 %collective-permute-start.1 = (bf16[48,1024]{1,0:T(8,128)(2,1)S(1)}, bf16[48,1024]{1,0:T(8,128)(2,1)S(1)}, u32[]{:S(2)}, u32[]{:S(2)}) collective-permute-start(bf16[48,1024]{1,0:T(8,128)(2,1)S(1)} %broadcast_select_fusion.4), channel_id=1, source_target_pairs={{0,16},{1,17},{2,18},{3,19},{4,20},{5,21},{6,22},{7,23},{8,24},{9,... | collective-permute-start | bytes 294920 | tf_op jit(solution)/shard_map/while/body/eval_jaxpr/ppermute | solution.py:10
  316.9 9.8 %collective-permute-start = (bf16[48,1024]{1,0:T(8,128)(2,1)S(1)}, bf16[48,1024]{1,0:T(8,128)(2,1)S(1)}, u32[]{:S(2)}, u32[]{:S(2)}) collective-permute-start(bf16[48,1024]{1,0:T(8,128)(2,1)S(1)} %broadcast_select_fusion.4), channel_id=1, source_target_pairs={{0,2},{2,4},{4,6},{6,8},{8,10},{10,12},{12,14},{1,3},{3,5},{5,7},{... | collective-permute-start | bytes 294920 | tf_op jit(solution)/shard_map/while/body/eval_jaxpr/ppermute | solution.py:10
  330.7 27.3 %reduce-scatter.2.cloned.1.call-start = ((), (), s32[]{:S(2)}) async-start(), calls=%async_computation.1 | async-start | bytes 589824 | tf_op jit(solution)/shard_map/while/body/eval_jaxpr/reduce_scatter | solution.py:46
  359.0 29.7 %reduce-scatter.2.cloned.1.call-start = ((), (), s32[]{:S(2)}) async-start(), calls=%async_computation.1 | async-start | bytes 589824 | tf_op jit(solution)/shard_map/while/body/eval_jaxpr/reduce_scatter | solution.py:46
  360.4 9.8 %collective-permute-start.2 = (bf16[48,1024]{1,0:T(8,128)(2,1)S(1)}, bf16[48,1024]{1,0:T(8,128)(2,1)S(1)}, u32[]{:S(2)}, u32[]{:S(2)}) collective-permute-start(bf16[48,1024]{1,0:T(8,128)(2,1)S(1)} %broadcast_select_fusion.5), channel_id=1, source_target_pairs={{2,0},{4,2},{6,4},{8,6},{10,8},{12,10},{14,12},{3,1},{5,3},{7,5},{... | collective-permute-start | bytes 294920 | tf_op jit(solution)/shard_map/while/body/eval_jaxpr/ppermute | solution.py:10
  389.8 27.3 %reduce-scatter.2.cloned.1.call-start = ((), (), s32[]{:S(2)}) async-start(), calls=%async_computation.1 | async-start | bytes 589824 | tf_op jit(solution)/shard_map/while/body/eval_jaxpr/reduce_scatter | solution.py:46
  418.1 23.7 %reduce-scatter.2.cloned.1.call-start = ((), (), s32[]{:S(2)}) async-start(), calls=%async_computation.1 | async-start | bytes 589824 | tf_op jit(solution)/shard_map/while/body/eval_jaxpr/reduce_scatter | solution.py:46
  442.9 23.7 %reduce-scatter.2.cloned.1.call-start = ((), (), s32[]{:S(2)}) async-start(), calls=%async_computation.1 | async-start | bytes 589824 | tf_op jit(solution)/shard_map/while/body/eval_jaxpr/reduce_scatter | solution.py:46
  (74 other events, 419.9 us)
Sparse Core Ops, SparseCore 0:
  17.4 11.6 reduce-scatter.1
  45.4 9.3 reduce-scatter.1
  70.8 11.7 reduce-scatter.1
  99.1 11.1 reduce-scatter.1
  127.5 10.7 reduce-scatter.1
  155.8 13.7 reduce-scatter.1
  186.8 14.0 reduce-scatter.1
  218.7 13.4 reduce-scatter.1
  253.0 10.4 reduce-scatter.1
  284.3 10.4 reduce-scatter.1
  312.1 14.0 reduce-scatter.1
  343.4 14.0 reduce-scatter.1
  374.1 11.0 reduce-scatter.1
  402.5 9.5 reduce-scatter.1
  430.9 8.1 reduce-scatter.1
  455.7 8.6 reduce-scatter.1
where the time goes:
time: 481 us; the launch traced here: 475 us
  starting transfers between devices  187 us (39%)
  waiting for transfers between devices  141 us (29%)
  matrix products  52.7 us (11%)
  other arithmetic  33 us (7%)
  blocking collectives  31.2 us (6%)
  between operations  13.8 us (3%)
  local copies, waits for them, and re-layouts  13.5 us (3%)
    ppermute x64, starting transfers between devices, shifted(): return lax.ppermute(shard, axis, pairs)  186 us
    ppermute x64, waiting for transfers between devices, shifted(): return lax.ppermute(shard, axis, pairs)  140 us
    dynamic_update_slice x32, other arithmetic, place(): lax.dynamic_update_slice_in_dim(result, kept, clamped * block_rows, 0)  31.8 us
    all_gather x16, blocking collectives, east_product(): segment = lax.all_gather(inflow, 'half', axis=1, tiled=True)  31.2 us
    dot_general x8, matrix products, east_product(): lax.dot_general(segment, matrix, (((1,), (1,)), ((), ())), preferred_elem...  28.5 us
    dot_general x8, matrix products, west_product(): jnp.dot(inflow, matrix, preferred_element_type=jnp.float32)  24.2 us
    while x32, local copies, waits for them, and re-layouts  11.9 us
  transfers between devices with their start and end apart: 80, of which 50 were waited for; matrix products, arithmetic and copies ran while one was open for 9% of the time, Pallas kernels for 0%

commit v1 on v0

v1 whole, which is shorter than its diff:
```python
import functools

import jax
import jax.numpy as jnp
from jax import lax
from jax.experimental import pallas as pl
from jax.experimental.pallas import tpu as pltpu
from jax.sharding import PartitionSpec as P

BLOCKS = 12
MESH = pl.DeviceIdType.MESH


def sweeps(rows, cols, op_ref, es_ref, ws_ref, eo_ref, wo_ref,
           op, op_t, es, ws, eout, wout, e_north, e_west, w_south, w_east,
           e_in, e_sib, w_part, w_sib, w_in, e_acc,
           load_sem, store_sem, send_sem, en_sem, ew_sem, wsn_sem, we_sem, esib_sem, wsib_sem):
    row, col, half = lax.axis_index("crow"), lax.axis_index("ccol"), lax.axis_index("half")
    blocks, block_rows, width = es.shape
    tile = min(256, width)
    east_level = row + col
    west_level = rows - 1 - row + cols - 1 - col
    has_n, has_s, has_w, has_e = row > 0, row < rows - 1, col > 0, col < cols - 1
    north, south = {"crow": row - 1}, {"crow": row + 1}
    west, east = {"ccol": col - 1}, {"ccol": col + 1}
    other = {"half": 1 - half}

    own = pl.multiple_of(half * width, width)
    theirs = pl.multiple_of((1 - half) * width, width)
    loads = [
        pltpu.make_async_copy(es_ref, es, load_sem.at[0]),
        pltpu.make_async_copy(ws_ref, ws, load_sem.at[1]),
        pltpu.make_async_copy(op_ref.at[:, pl.ds(own, width)], op.at[0], load_sem.at[2]),
        pltpu.make_async_copy(op_ref.at[:, pl.ds(theirs, width)], op.at[1], load_sem.at[3]),
    ]
    for load in loads:
        load.start()

    barrier = pltpu.get_barrier_semaphore()
    pl.semaphore_signal(barrier, inc=1, device_id=other, device_id_type=MESH)
    for there, who in ((has_n, north), (has_s, south), (has_w, west), (has_e, east)):
        @pl.when(there)
        def _():
            pl.semaphore_signal(barrier, inc=1, device_id=who, device_id_type=MESH)
    for there, buffer in ((has_n, e_north), (has_s, w_south), (has_w, e_west), (has_e, w_east)):
        @pl.when(jnp.logical_not(there))
        def _():
            buffer[...] = jnp.zeros_like(buffer)
    pl.semaphore_wait(
        barrier,
        1 + has_n.astype(jnp.int32) + has_s.astype(jnp.int32)
        + has_w.astype(jnp.int32) + has_e.astype(jnp.int32),
    )

    def remote(src, dst, send, recv, who):
        return pltpu.make_async_remote_copy(
            src_ref=src, dst_ref=dst, send_sem=send, recv_sem=recv,
            device_id=who, device_id_type=MESH)

    def to_south(src, k):
        return remote(src.at[k], e_north.at[k], send_sem.at[0], en_sem.at[k], south)

    def to_east(src, k):
        return remote(src.at[k], e_west.at[k], send_sem.at[1], ew_sem.at[k], east)

    def to_north(src, k):
        return remote(src.at[k], w_south.at[k], send_sem.at[2], wsn_sem.at[k], north)

    def to_west(src, k):
        return remote(src.at[k], w_east.at[k], send_sem.at[3], we_sem.at[k], west)

    def e_exchange(k):
        return remote(e_in.at[k], e_sib.at[k], send_sem.at[4], esib_sem.at[k], other)

    def w_exchange(k):
        return remote(w_part.at[k], w_sib.at[k], send_sem.at[5], wsib_sem.at[k], other)

    def send_east(src, k):
        @pl.when(has_e)
        def _():
            to_east(src, k).start()

        @pl.when(has_s)
        def _():
            to_south(src, k).start()
        pltpu.make_async_copy(src.at[k], eo_ref.at[k], store_sem.at[0]).start()

    def send_west(src, k):
        @pl.when(has_w)
        def _():
            to_west(src, k).start()

        @pl.when(has_n)
        def _():
            to_north(src, k).start()
        pltpu.make_async_copy(src.at[k], wo_ref.at[k], store_sem.at[1]).start()

    loads[0].wait()

    @pl.when(east_level == 0)
    def _():
        @pl.loop(0, blocks)
        def _(k):
            send_east(es, k)

    loads[1].wait()

    @pl.when(west_level == 0)
    def _():
        @pl.loop(0, blocks)
        def _(k):
            send_west(ws, k)

    loads[2].wait()
    loads[3].wait()

    @pl.when(east_level > 0)
    def _():
        @pl.loop(0, width // tile)
        def _(t):
            at = pl.multiple_of(t * tile, tile)
            for k in range(2):
                for n in range(0, width, tile):
                    op_t[k, pl.ds(at, tile), n:n + tile] = op[k, n:n + tile, pl.ds(at, tile)].T

    @pl.loop(0, rows + cols - 2 + blocks)
    def _(step):
        ek, wk = step - east_level, step - west_level
        e_on = (east_level > 0) & (ek >= 0) & (ek < blocks)
        w_on = (west_level > 0) & (wk >= 0) & (wk < blocks)

        @pl.when(e_on)
        def _():
            @pl.when(has_n)
            def _():
                to_south(eout, ek).wait_recv()

            @pl.when(has_w)
            def _():
                to_east(eout, ek).wait_recv()
            e_in[ek] = (e_north[ek].astype(jnp.float32) + e_west[ek].astype(jnp.float32)).astype(jnp.bfloat16)
            e_exchange(ek).start()

        @pl.when(w_on)
        def _():
            @pl.when(has_s)
            def _():
                to_north(wout, wk).wait_recv()

            @pl.when(has_e)
            def _():
                to_west(wout, wk).wait_recv()
            w_in[...] = (w_south[wk].astype(jnp.float32) + w_east[wk].astype(jnp.float32)).astype(jnp.bfloat16)
            for n in range(0, width, tile):
                w_part[wk, :, n:n + tile] = jnp.dot(
                    w_in[...], op[1, :, n:n + tile], preferred_element_type=jnp.float32).astype(jnp.bfloat16)
            w_exchange(wk).start()

        @pl.when(e_on)
        def _():
            for n in range(0, width, tile):
                e_acc[:, n:n + tile] = es[ek, :, n:n + tile].astype(jnp.float32) + jnp.dot(
                    e_in[ek], op_t[0, :, n:n + tile], preferred_element_type=jnp.float32)
            e_exchange(ek).wait_recv()
            for n in range(0, width, tile):
                eout[ek, :, n:n + tile] = (e_acc[:, n:n + tile] + jnp.dot(
                    e_sib[ek], op_t[1, :, n:n + tile], preferred_element_type=jnp.float32)).astype(jnp.bfloat16)
            send_east(eout, ek)

        @pl.when(w_on)
        def _():
            for n in range(0, width, tile):
                e_acc[:, n:n + tile] = ws[wk, :, n:n + tile].astype(jnp.float32) + jnp.dot(
                    w_in[...], op[0, :, n:n + tile], preferred_element_type=jnp.float32)
            w_exchange(wk).wait_recv()
            wout[wk] = (e_acc[...] + w_sib[wk].astype(jnp.float32)).astype(jnp.bfloat16)
            send_west(wout, wk)

    for there, src, dst, send, recv, who in (
        (has_s, eout, e_north, 0, en_sem, south),
        (has_e, eout, e_west, 1, ew_sem, east),
        (has_n, wout, w_south, 2, wsn_sem, north),
        (has_w, wout, w_east, 3, we_sem, west),
        (east_level > 0, e_in, e_sib, 4, esib_sem, other),
        (west_level > 0, w_part, w_sib, 5, wsib_sem, other),
    ):
        @pl.when(there)
        def _():
            remote(src, dst, send_sem.at[send], recv.at[0], who).wait_send()
    pltpu.make_async_copy(eout, eo_ref, store_sem.at[0]).wait()
    pltpu.make_async_copy(wout, wo_ref, store_sem.at[1]).wait()


def local(rows, cols, operator, east_sources, west_sources):
    matrix = operator[0, 0]
    batch, width = east_sources.shape[2:]
    blocks, block_rows = BLOCKS, batch // BLOCKS
    cut = (blocks, block_rows, width)
    any_space = pl.BlockSpec(memory_space=pl.ANY)
    trace = pltpu.VMEM(cut, jnp.bfloat16)
    weights = pltpu.VMEM((2, width, width), jnp.bfloat16)
    east, west = pl.pallas_call(
        functools.partial(sweeps, rows, cols),
        out_shape=[jax.ShapeDtypeStruct(cut, jnp.bfloat16)] * 2,
        in_specs=[any_space] * 3,
        out_specs=[any_space] * 2,
        scratch_shapes=[weights, weights] + [trace] * 12 + [
            pltpu.VMEM((block_rows, width), jnp.bfloat16),
            pltpu.VMEM((block_rows, width), jnp.float32),
            pltpu.SemaphoreType.DMA((4,)),
            pltpu.SemaphoreType.DMA((2,)),
            pltpu.SemaphoreType.DMA((6,)),
        ] + [pltpu.SemaphoreType.DMA((blocks,))] * 6,
        compiler_params=pltpu.CompilerParams(
            collective_id=0, has_side_effects=True, vmem_limit_bytes=40 * 2**20),
        name="sweeps",
    )(matrix, east_sources.reshape(cut), west_sources.reshape(cut))
    return east.reshape(1, 1, batch, width), west.reshape(1, 1, batch, width)


def solution(mesh):
    in_specs = (
        P("crow", "ccol", "half", None),
        P("crow", "ccol", None, "half"),
        P("crow", "ccol", None, "half"),
    )
    out_specs = (P("crow", "ccol", None, "half"), P("crow", "ccol", None, "half"))
    body = functools.partial(local, mesh.shape["crow"], mesh.shape["ccol"])
    return jax.shard_map(body, mesh=mesh, in_specs=in_specs, out_specs=out_specs, check_vma=False)
```

time: 481 us -> 125 us (0.26); the launches traced: 475 us -> 125 us
  starting transfers between devices: 187 us -> 0 us
  waiting for transfers between devices: 141 us -> 0 us
  Pallas kernels: 0 us -> 118 us
  matrix products: 52.7 us -> 0 us
  other arithmetic: 33 us -> 0 us
  blocking collectives: 31.2 us -> 0 us
  between operations: 13.8 us -> 0.65 us
  local copies, waits for them, and re-layouts: 13.5 us -> 6.21 us
    ppermute x64 -> x0, starting transfers between devices: 186 us -> none  [shifted(): return lax.ppermute(shard, axis, pairs)]
    ppermute x64 -> x0, waiting for transfers between devices: 140 us -> none  [shifted(): return lax.ppermute(shard, axis, pairs)]
    pallas_call x0 -> x1, Pallas kernels: none -> 118 us  [local(): pl.pallas_call(functools.partial(sweeps, rows, cols), out_shape=[jax.Shap...]
    dot_general x16 -> x0, matrix products: 52.7 us -> none  [the longest x8 28.5 us: east_product(): lax.dot_general(segment, matrix, (((1,), (1,)), ((), ())), preferred_elem...]
    dynamic_update_slice x32 -> x0, other arithmetic: 31.8 us -> none  [place(): lax.dynamic_update_slice_in_dim(result, kept, clamped * block_rows, 0)]
    all_gather x16 -> x0, blocking collectives: 31.2 us -> none  [east_product(): segment = lax.all_gather(inflow, 'half', axis=1, tiled=True)]
    while x32 -> x0, local copies, waits for them, and re-layouts: 11.9 us -> none
    unnamed x4 -> x8, local copies, waits for them, and re-layouts: 1.12 us -> 6.21 us
  transfers between devices with their start and end apart: 80 -> 0, of which waited for: 50 -> 0; matrix products, arithmetic and copies ran while one was open for 9% -> 0% of each run, Pallas kernels for 0% -> 0%
where the time goes in v1:
time: 125 us
  Pallas kernels  118 us (94%)
  local copies, waits for them, and re-layouts  6.21 us (5%)
    pallas_call x1, Pallas kernels, local(): pl.pallas_call(functools.partial(sweeps, rows, cols), out_shape=[jax.Shap...  118 us
    unnamed x8, local copies, waits for them, and re-layouts  6.21 us

profile of v1, /device:TPU:0, one launch (start us, length us, event | category | flops | bytes accessed | tf_op | source)
XLA Modules:
  0.0 124.9 jit_solution(14019017219454145466)
XLA Ops:
  0.6 0.0 copy-start
  0.6 2.2 %copy-done = bf16[1,1,1024,2048]{3,2,1,0:T(8,128)(2,1)S(1)} copy-done((bf16[1,1,1024,2048]{3,2,1,0:T(8,128)(2,1)S(1)}, bf16[1,1,1024,2048]{3,2,1,0:T(8,128)(2,1)}, u32[]{:S(2)}) %copy-start) | copy-done | bytes 4194328
  2.8 0.0 copy-start.1
  2.8 1.1 copy-done.1
  4.0 0.0 copy-start.2
  4.0 1.1 copy-done.2
  5.1 118.0 %sweeps.1 = (bf16[12,32,1024]{2,1,0:T(8,128)(2,1)S(1)}, bf16[12,32,1024]{2,1,0:T(8,128)(2,1)S(1)}) custom-call(bf16[1024,2048]{1,0:T(8,128)(2,1)S(1)} %bitcast.5, bf16[12,32,1024]{2,1,0:T(8,128)(2,1)S(1)} %bitcast.8, bf16[12,32,1024]{2,1,0:T(8,128)(2,1)S(1)} %bitcast.9), custom_call_target="tpu_custom_call" | custom-call | tf_op jit(solution)/shard_map/sweeps/pallas_call | solution.py:202
  123.1 0.9 copy.7
  124.0 0.9 copy.8
Async XLA Ops:
  0.6 2.2 %copy-start = (bf16[1,1,1024,2048]{3,2,1,0:T(8,128)(2,1)S(1)}, bf16[1,1,1024,2048]{3,2,1,0:T(8,128)(2,1)}, u32[]{:S(2)}) copy-start(bf16[1,1,1024,2048]{3,2,1,0:T(8,128)(2,1)} %param.3) | copy-start | bytes 12582916
  2.8 1.1 copy-start.1
  4.0 1.1 copy-start.2

commit v2 on v1

--- a/solution.py
+++ b/solution.py
@@ -8,6 +8,7 @@
 from jax.sharding import PartitionSpec as P
 
 BLOCKS = 12
+SKEW = 4
 MESH = pl.DeviceIdType.MESH
 
 
@@ -123,9 +124,9 @@
                 for n in range(0, width, tile):
                     op_t[k, pl.ds(at, tile), n:n + tile] = op[k, n:n + tile, pl.ds(at, tile)].T
 
-    @pl.loop(0, rows + cols - 2 + blocks)
+    @pl.loop(0, SKEW * (rows + cols - 2) + blocks)
     def _(step):
-        ek, wk = step - east_level, step - west_level
+        ek, wk = step - SKEW * east_level, step - SKEW * west_level
         e_on = (east_level > 0) & (ek >= 0) & (ek < blocks)
         w_on = (west_level > 0) & (wk >= 0) & (wk < blocks)
 
@@ -212,7 +213,7 @@
             pltpu.SemaphoreType.DMA((6,)),
         ] + [pltpu.SemaphoreType.DMA((blocks,))] * 6,
         compiler_params=pltpu.CompilerParams(
-            collective_id=0, has_side_effects=True, vmem_limit_bytes=40 * 2**20),
+            collective_id=0, has_side_effects=True, vmem_limit_bytes=63 * 2**20),
         name="sweeps",
     )(matrix, east_sources.reshape(cut), west_sources.reshape(cut))
     return east.reshape(1, 1, batch, width), west.reshape(1, 1, batch, width)

time: 125 us -> 85.4 us (0.68)
  Pallas kernels: 118 us -> 80.4 us
  local copies, waits for them, and re-layouts: 6.21 us -> 4.13 us
    pallas_call x1, Pallas kernels: 118 us -> 80.4 us  [local(): pl.pallas_call(functools.partial(sweeps, rows, cols), out_shape=[jax.Shap...]
    unnamed x8 -> x2, local copies, waits for them, and re-layouts: 6.21 us -> 4.13 us
where the time goes in v2:
time: 85.4 us; the launch traced here: 85.2 us
  Pallas kernels  80.4 us (94%)
  local copies, waits for them, and re-layouts  4.13 us (5%)
    pallas_call x1, Pallas kernels, local(): pl.pallas_call(functools.partial(sweeps, rows, cols), out_shape=[jax.Shap...  80.4 us
    unnamed x2, local copies, waits for them, and re-layouts  4.13 us

profile of v2, /device:TPU:0, one launch (start us, length us, event | category | flops | bytes accessed | tf_op | source)
XLA Modules:
  0.0 85.2 jit_solution(11954174479192359567)
XLA Ops:
  0.6 80.4 %sweeps.1 = (bf16[12,32,1024]{2,1,0:T(8,128)(2,1)}, bf16[12,32,1024]{2,1,0:T(8,128)(2,1)}) custom-call(bf16[1024,2048]{1,0:T(8,128)(2,1)} %bitcast.5, bf16[12,32,1024]{2,1,0:T(8,128)(2,1)} %bitcast.8, bf16[12,32,1024]{2,1,0:T(8,128)(2,1)} %bitcast.9), custom_call_target="tpu_custom_call" | custom-call | tf_op jit(solution)/shard_map/sweeps/pallas_call | solution.py:203
  81.1 2.1 %copy.7 = bf16[1,1,384,1024]{3,2,1,0:T(8,128)(2,1)} copy(bf16[1,1,384,1024]{3,2,1,0:T(8,128)(2,1)} %bitcast.7) | data formatting | bytes 1572864
  83.1 2.1 %copy.8 = bf16[1,1,384,1024]{3,2,1,0:T(8,128)(2,1)} copy(bf16[1,1,384,1024]{3,2,1,0:T(8,128)(2,1)} %bitcast.6) | data formatting | bytes 1572864

commit v3 on v2

--- a/solution.py
+++ b/solution.py
@@ -7,15 +7,17 @@
 from jax.experimental.pallas import tpu as pltpu
 from jax.sharding import PartitionSpec as P
 
-BLOCKS = 12
+BLOCKS = 8
 SKEW = 4
+DIRECT = 3
+LAG = 2
 MESH = pl.DeviceIdType.MESH
 
 
 def sweeps(rows, cols, op_ref, es_ref, ws_ref, eo_ref, wo_ref,
            op, op_t, es, ws, eout, wout, e_north, e_west, w_south, w_east,
-           e_in, e_sib, w_part, w_sib, w_in, e_acc,
-           load_sem, store_sem, send_sem, en_sem, ew_sem, wsn_sem, we_sem, esib_sem, wsib_sem):
+           e_in, e_sib, w_part, w_sib, e_relay, w_relay, w_in, e_acc,
+           load_sem, store_sem, send_sem, en_sem, ew_sem, wsn_sem, we_sem, esib_sem, wsib_sem, er_sem, wr_sem):
     row, col, half = lax.axis_index("crow"), lax.axis_index("ccol"), lax.axis_index("half")
     blocks, block_rows, width = es.shape
     tile = min(256, width)
@@ -25,6 +27,12 @@
     north, south = {"crow": row - 1}, {"crow": row + 1}
     west, east = {"ccol": col - 1}, {"ccol": col + 1}
     other = {"half": 1 - half}
+
+    mid, last = cols // 2, cols - 1
+    detour = mid >= 2
+    e_from, e_via = detour & (col == mid - 1), detour & (col == 0)
+    w_from, w_via = detour & (col == mid), detour & (col == last)
+    at_mid, at_end = e_from | w_from, e_via | w_via
 
     own = pl.multiple_of(half * width, width)
     theirs = pl.multiple_of((1 - half) * width, width)
@@ -43,6 +51,11 @@
         @pl.when(there)
         def _():
             pl.semaphore_signal(barrier, inc=1, device_id=who, device_id_type=MESH)
+    for there, whos in ((at_mid, (0, last)), (at_end, (mid - 1, mid))):
+        @pl.when(there)
+        def _():
+            for who in whos:
+                pl.semaphore_signal(barrier, inc=1, device_id={"ccol": who}, device_id_type=MESH)
     for there, buffer in ((has_n, e_north), (has_s, w_south), (has_w, e_west), (has_e, w_east)):
         @pl.when(jnp.logical_not(there))
         def _():
@@ -50,7 +63,8 @@
     pl.semaphore_wait(
         barrier,
         1 + has_n.astype(jnp.int32) + has_s.astype(jnp.int32)
-        + has_w.astype(jnp.int32) + has_e.astype(jnp.int32),
+        + has_w.astype(jnp.int32) + has_e.astype(jnp.int32)
+        + 2 * at_mid.astype(jnp.int32) + 2 * at_end.astype(jnp.int32),
     )
 
     def remote(src, dst, send, recv, who):
@@ -76,8 +90,26 @@
     def w_exchange(k):
         return remote(w_part.at[k], w_sib.at[k], send_sem.at[5], wsib_sem.at[k], other)
 
+    def e_out(k):
+        return remote(eout.at[k], e_relay.at[k], send_sem.at[1], er_sem.at[k], {"ccol": 0})
+
+    def e_on_to(k):
+        return remote(e_relay.at[k], e_west.at[k], send_sem.at[6], ew_sem.at[k], {"ccol": mid})
+
+    def w_out(k):
+        return remote(wout.at[k], w_relay.at[k], send_sem.at[3], wr_sem.at[k], {"ccol": last})
+
+    def w_on_to(k):
+        return remote(w_relay.at[k], w_east.at[k], send_sem.at[7], we_sem.at[k], {"ccol": mid - 1})
+
     def send_east(src, k):
-        @pl.when(has_e)
+        far = e_from & (k >= DIRECT)
+        if detour and src is eout:
+            @pl.when(far)
+            def _():
+                e_out(k).start()
+
+        @pl.when(has_e & jnp.logical_not(far))
         def _():
             to_east(src, k).start()
 
@@ -87,7 +119,13 @@
         pltpu.make_async_copy(src.at[k], eo_ref.at[k], store_sem.at[0]).start()
 
     def send_west(src, k):
-        @pl.when(has_w)
+        far = w_from & (k >= DIRECT)
+        if detour and src is wout:
+            @pl.when(far)
+            def _():
+                w_out(k).start()
+
+        @pl.when(has_w & jnp.logical_not(far))
         def _():
             to_west(src, k).start()
 
@@ -129,6 +167,20 @@
         ek, wk = step - SKEW * east_level, step - SKEW * west_level
         e_on = (east_level > 0) & (ek >= 0) & (ek < blocks)
         w_on = (west_level > 0) & (wk >= 0) & (wk < blocks)
+
+        if detour:
+            er = step - SKEW * (row + mid - 1) - LAG
+            wr = step - SKEW * (rows - 1 - row + last - mid) - LAG
+
+            @pl.when(e_via & (er >= DIRECT) & (er < blocks))
+            def _():
+                e_out(er).wait_recv()
+                e_on_to(er).start()
+
+            @pl.when(w_via & (wr >= DIRECT) & (wr < blocks))
+            def _():
+                w_out(wr).wait_recv()
+                w_on_to(wr).start()
 
         @pl.when(e_on)
         def _():
@@ -188,6 +240,14 @@
         @pl.when(there)
         def _():
             remote(src, dst, send_sem.at[send], recv.at[0], who).wait_send()
+    if detour and DIRECT < blocks:
+        for there, src, dst, send, recv, who in (
+            (e_via, e_relay, e_west, 6, ew_sem, mid), (w_via, w_relay, w_east, 7, we_sem, mid - 1),
+        ):
+            @pl.when(there)
+            def _():
+                some = pl.ds(DIRECT, blocks - DIRECT)
+                remote(src.at[some], dst.at[some], send_sem.at[send], recv.at[0], {"ccol": who}).wait_send()
     pltpu.make_async_copy(eout, eo_ref, store_sem.at[0]).wait()
     pltpu.make_async_copy(wout, wo_ref, store_sem.at[1]).wait()
 
@@ -205,13 +265,13 @@
         out_shape=[jax.ShapeDtypeStruct(cut, jnp.bfloat16)] * 2,
         in_specs=[any_space] * 3,
         out_specs=[any_space] * 2,
-        scratch_shapes=[weights, weights] + [trace] * 12 + [
+        scratch_shapes=[weights, weights] + [trace] * 14 + [
             pltpu.VMEM((block_rows, width), jnp.bfloat16),
             pltpu.VMEM((block_rows, width), jnp.float32),
             pltpu.SemaphoreType.DMA((4,)),
             pltpu.SemaphoreType.DMA((2,)),
-            pltpu.SemaphoreType.DMA((6,)),
-        ] + [pltpu.SemaphoreType.DMA((blocks,))] * 6,
+            pltpu.SemaphoreType.DMA((8,)),
+        ] + [pltpu.SemaphoreType.DMA((blocks,))] * 8,
         compiler_params=pltpu.CompilerParams(
             collective_id=0, has_side_effects=True, vmem_limit_bytes=63 * 2**20),
         name="sweeps",

time: 85.4 us -> 83.9 us (0.982)
  Pallas kernels: 80.4 us -> 79 us
    pallas_call x1, Pallas kernels: 80.4 us -> 79 us  [local(): pl.pallas_call(functools.partial(sweeps, rows, cols), out_shape=[jax.Shap...]
where the time goes in v3:
time: 83.9 us; the launch traced here: 83.7 us
  Pallas kernels  79 us (94%)
  local copies, waits for them, and re-layouts  4.13 us (5%)
    pallas_call x1, Pallas kernels, local(): pl.pallas_call(functools.partial(sweeps, rows, cols), out_shape=[jax.Shap...  79 us
    unnamed x2, local copies, waits for them, and re-layouts  4.13 us

profile of v3, /device:TPU:0, one launch (start us, length us, event | category | flops | bytes accessed | tf_op | source)
XLA Modules:
  0.0 83.7 jit_solution(12120650851217781773)
XLA Ops:
  0.6 79.0 %sweeps.1 = (bf16[8,48,1024]{2,1,0:T(8,128)(2,1)}, bf16[8,48,1024]{2,1,0:T(8,128)(2,1)}) custom-call(bf16[1024,2048]{1,0:T(8,128)(2,1)} %bitcast.5, bf16[8,48,1024]{2,1,0:T(8,128)(2,1)} %bitcast.8, bf16[8,48,1024]{2,1,0:T(8,128)(2,1)} %bitcast.9), custom_call_target="tpu_custom_call" | custom-call | tf_op jit(solution)/shard_map/sweeps/pallas_call | solution.py:263
  79.6 2.1 %copy.7 = bf16[1,1,384,1024]{3,2,1,0:T(8,128)(2,1)} copy(bf16[1,1,384,1024]{3,2,1,0:T(8,128)(2,1)} %bitcast.7) | data formatting | bytes 1572864
  81.7 2.1 %copy.8 = bf16[1,1,384,1024]{3,2,1,0:T(8,128)(2,1)} copy(bf16[1,1,384,1024]{3,2,1,0:T(8,128)(2,1)} %bitcast.6) | data formatting | bytes 1572864
